TPU v7x, 32 devices: a whole 2x2x4 slice. The times are simulated.
32 devices in a mesh: dp: 8 (over z, y), tensor: 4 (over x, core).
Axes of the slice: x: 2, y: 2, z: 4, core: 2. Of those that a mesh axis runs over, the one named last changes fastest.
Arguments:
- tokens: bfloat16 [8192, 1024], P(('dp', 'tensor')), may hold values from -6 to 6
- cotangent: float32 [8192, 1024], P(('dp', 'tensor')), may hold values from -6 to 6
- lengths: int32 [8, 2], P('dp'), may hold values from 64 to 512, as said below
- order: int32 [8, 1024], P('dp'), may hold values from 0 to 1023, each once within a row
- adapter_ids: int32 [8, 2], P('dp'), may hold values from 0 to 7
- norm1_gain: float32 [1024], replicated, may hold values from 0.25 to 1.75
- norm1_shift: float32 [1024], replicated, may hold values from -1.5 to 1.5
- qkv_weight: bfloat16 [1024, 3, 1024], P(None, None, 'tensor'), may hold values from -0.1875 to 0.1875
- qv_bias: float32 [2, 1024], P(None, 'tensor'), may hold values from -1.5 to 1.5
- proj_weight: bfloat16 [1024, 1024], P('tensor'), may hold values from -1.5 to 1.5
- proj_bias: float32 [1024], replicated, may hold values from -1.5 to 1.5
- norm2_gain: float32 [1024], replicated, may hold values from 0.25 to 1.75
- norm2_shift: float32 [1024], replicated, may hold values from -1.5 to 1.5
- up_weight: bfloat16 [1024, 4096], P(None, 'tensor'), may hold values from -0.1875 to 0.1875
- up_bias: float32 [4096], P('tensor'), may hold values from -1.5 to 1.5
- down_weight: bfloat16 [4096, 1024], P('tensor'), may hold values from -0.09375 to 0.09375
- down_bias: float32 [1024], replicated, may hold values from -1.5 to 1.5
- adapt_qkv_in: bfloat16 [1024, 128], replicated, may hold values from -0.1875 to 0.1875
- adapt_qkv_out: bfloat16 [128, 3, 1024], P(None, None, 'tensor'), may hold values from -0.75 to 0.75
- adapt_proj_in: bfloat16 [1024, 128], P('tensor'), may hold values from -0.75 to 0.75
- adapt_proj_out: bfloat16 [128, 1024], replicated, may hold values from -0.75 to 0.75
- adapt_up_in: bfloat16 [1024, 128], replicated, may hold values from -0.1875 to 0.1875
- adapt_up_out: bfloat16 [128, 4096], P(None, 'tensor'), may hold values from -0.75 to 0.75
- adapt_down_in: bfloat16 [4096, 128], P('tensor'), may hold values from -0.09375 to 0.09375
- adapt_down_out: bfloat16 [128, 1024], replicated, may hold values from -0.75 to 0.75
Outputs:
- result: float32 [8192, 1024], P(('dp', 'tensor'))
- grad_input: float32 [8192, 1024], P(('dp', 'tensor'))
- grad_qkv_in: float32 [1024, 128], replicated
- grad_qkv_out: float32 [128, 3, 1024], P(None, None, 'tensor')
- grad_proj_in: float32 [1024, 128], P('tensor')
- grad_proj_out: float32 [128, 1024], replicated
- grad_up_in: float32 [1024, 128], replicated
- grad_up_out: float32 [128, 4096], P(None, 'tensor')
- grad_down_in: float32 [4096, 128], P('tensor')
- grad_down_out: float32 [128, 1024], replicated
Inputs may be any that keep to these rules, and one draw needn't show every extreme that they name: `lengths`: in every group one sequence has exactly 512 valid tokens; the others have at least 512 // 8 (and at least one). `order`: each row is a permutation of the group's 1024 stored rows.
All inputs are finite; a program needn't handle non-finite values.
Results may differ from a plain program's by a relative error of at most 0.023.
Values may be sent and summed in bfloat16 or wider, within the bound.
No kernel may reach another device: no remote copies, remote signals or barrier semaphores. Data moves between devices by JAX's collectives and lax.ppermute only.
A program may use at most 128 MiB of HBM per device.

v0:
```python
import math
import jax
import jax.numpy as jnp
from jax import lax
from jax.sharding import PartitionSpec as P

D = 1024
HD = 64
RANK = 16
EPSILON = 1e-05
NEGATIVE = -1000000000.0


def layer_norm(values, gain, shift):
    centre = values - jnp.mean(values, -1, keepdims=True)
    spread = jnp.mean(centre * centre, -1, keepdims=True)
    return centre * lax.rsqrt(spread + EPSILON) * gain + shift


def matmul(left, right):
    return jnp.dot(left, right, preferred_element_type=jnp.float32)


def matmul_back(left, right):
    return lax.dot_general(
        left, right, (((1,), (1,)), ((), ())), preferred_element_type=jnp.float32
    )


def matmul_over(left, right):
    return lax.dot_general(
        left, right, (((0,), (0,)), ((), ())), preferred_element_type=jnp.float32
    )


def gelu_tanh(values):
    return jax.nn.gelu(values, approximate=True)


def block_scores(queries, keys, query_start, length):
    scale = 1.0 / math.sqrt(HD)
    scores = jnp.einsum("qhc,khc->hqk", queries, keys, preferred_element_type=jnp.float32) * scale
    query_pos = query_start + jnp.arange(queries.shape[0], dtype=jnp.int32)
    key_pos = jnp.arange(keys.shape[0], dtype=jnp.int32)
    allowed = (key_pos[None, :] <= query_pos[:, None]) & (key_pos[None, :] < length)
    return jnp.where(allowed[None], scores, NEGATIVE)


def attention_forward(qkv_seq, lengths_row, seq_len):
    group_rows = qkv_seq.shape[0]
    heads_here = qkv_seq.shape[2] // HD
    block_rows = min(512, seq_len)
    per_seq = seq_len // block_rows
    split = qkv_seq.reshape(group_rows, 3, heads_here, HD)

    def one_block(block_id):
        seq_id = block_id // per_seq
        query_start = block_id % per_seq * block_rows
        base = seq_id * seq_len
        queries = lax.dynamic_slice_in_dim(split[:, 0], base + query_start, block_rows, 0)
        keys = lax.dynamic_slice_in_dim(split[:, 1], base, seq_len, 0)
        values = lax.dynamic_slice_in_dim(split[:, 2], base, seq_len, 0)
        scores = block_scores(queries, keys, query_start, lengths_row[seq_id])
        top = jnp.max(scores, -1, keepdims=True)
        weights = jnp.exp(scores - top)
        total = jnp.sum(weights, -1, keepdims=True)
        probs = (weights / total).astype(jnp.bfloat16)
        attended = jnp.einsum("hqk,khc->qhc", probs, values, preferred_element_type=jnp.float32)
        return (attended.reshape(block_rows, heads_here * HD), (top + jnp.log(total))[..., 0])

    blocks = group_rows // block_rows
    outputs, log_totals = lax.map(one_block, jnp.arange(blocks, dtype=jnp.int32))
    return (outputs.reshape(group_rows, heads_here * HD), log_totals)


def attention_backward(qkv_seq, grad_seq, log_totals, lengths_row, seq_len):
    group_rows = qkv_seq.shape[0]
    heads_here = qkv_seq.shape[2] // HD
    block_rows = min(512, seq_len)
    per_seq = seq_len // block_rows
    seqs = group_rows // seq_len
    scale = 1.0 / math.sqrt(HD)
    split = qkv_seq.reshape(group_rows, 3, heads_here, HD)
    grad_split = grad_seq.reshape(group_rows, heads_here, HD)

    def one_block(block_id):
        seq_id = block_id // per_seq
        query_start = block_id % per_seq * block_rows
        base = seq_id * seq_len
        queries = lax.dynamic_slice_in_dim(split[:, 0], base + query_start, block_rows, 0)
        keys = lax.dynamic_slice_in_dim(split[:, 1], base, seq_len, 0)
        values = lax.dynamic_slice_in_dim(split[:, 2], base, seq_len, 0)
        grad_block = lax.dynamic_slice_in_dim(grad_split, base + query_start, block_rows, 0)
        scores = block_scores(queries, keys, query_start, lengths_row[seq_id])
        probs = jnp.exp(scores - log_totals[block_id][..., None])
        grad_probs = jnp.einsum(
            "qhc,khc->hqk", grad_block, values, preferred_element_type=jnp.float32
        )
        centre = jnp.sum(probs * grad_probs, -1, keepdims=True)
        grad_raw = (probs * (grad_probs - centre) * scale).astype(jnp.bfloat16)
        grad_query = jnp.einsum("hqk,khc->qhc", grad_raw, keys, preferred_element_type=jnp.float32)
        grad_key = jnp.einsum("hqk,qhc->khc", grad_raw, queries, preferred_element_type=jnp.float32)
        grad_value = jnp.einsum(
            "hqk,qhc->khc",
            probs.astype(jnp.bfloat16),
            grad_block,
            preferred_element_type=jnp.float32,
        )
        return (grad_query, grad_key, grad_value)

    blocks = group_rows // block_rows
    grad_query, grad_key, grad_value = lax.map(one_block, jnp.arange(blocks, dtype=jnp.int32))
    width_here = heads_here * HD
    grad_query = grad_query.reshape(group_rows, width_here)
    grad_key = jnp.sum(grad_key.reshape(seqs, per_seq, seq_len, width_here), axis=1).reshape(
        group_rows, width_here
    )
    grad_value = jnp.sum(grad_value.reshape(seqs, per_seq, seq_len, width_here), axis=1).reshape(
        group_rows, width_here
    )
    return jnp.stack([grad_query, grad_key, grad_value], 1)


def body(
    tokens,
    cotangent,
    lengths,
    order,
    adapter_ids,
    norm1_gain,
    norm1_shift,
    qkv_weight,
    qv_bias,
    proj_weight,
    proj_bias,
    norm2_gain,
    norm2_shift,
    up_weight,
    up_bias,
    down_weight,
    down_bias,
    adapt_qkv_in,
    adapt_qkv_out,
    adapt_proj_in,
    adapt_proj_out,
    adapt_up_in,
    adapt_up_out,
    adapt_down_in,
    adapt_down_out,
):
    own_rows = tokens.shape[0]
    order_row = order[0]
    lengths_row = lengths[0]
    ids_row = adapter_ids[0]
    group_rows = order_row.shape[0]
    seqs = lengths_row.shape[0]
    seq_len = group_rows // seqs
    adapt_cols = adapt_qkv_in.shape[1]
    rank_index = lax.axis_index("tensor")
    inverse = (
        jnp.zeros((group_rows,), jnp.int32)
        .at[order_row]
        .set(jnp.arange(group_rows, dtype=jnp.int32))
    )
    seq_of = inverse // seq_len
    adapter_of = jnp.sum(
        jnp.where(
            seq_of[:, None] == jnp.arange(seqs, dtype=jnp.int32)[None, :], ids_row[None, :], 0
        ),
        axis=1,
    )
    group_mask = (
        jnp.arange(adapt_cols, dtype=jnp.int32)[None, :] // RANK == adapter_of[:, None]
    ).astype(jnp.float32)
    own_mask = lax.dynamic_slice_in_dim(group_mask, rank_index * own_rows, own_rows, 0)
    bias_three = jnp.stack([qv_bias[0], jnp.zeros_like(qv_bias[0]), qv_bias[1]])
    proj_joined = jnp.concatenate([proj_weight, adapt_proj_in], 1)
    down_joined = jnp.concatenate([down_weight, adapt_down_in], 1)
    up_joined = jnp.concatenate([up_weight, adapt_up_out], 0)
    qkv_joined = jnp.concatenate([qkv_weight, adapt_qkv_out], 0)

    def project_qkv(rows_all, lowrank_all):
        value = jnp.einsum("rd,dkc->rkc", rows_all, qkv_weight, preferred_element_type=jnp.float32)
        value = value + jnp.einsum(
            "ra,akc->rkc", lowrank_all, adapt_qkv_out, preferred_element_type=jnp.float32
        )
        return (value + bias_three[None]).astype(jnp.bfloat16)

    def project_up(rows_all, lowrank_all):
        return matmul(rows_all, up_weight) + matmul(lowrank_all, adapt_up_out) + up_bias

    inputs = tokens.astype(jnp.float32)
    normed1 = layer_norm(inputs, norm1_gain, norm1_shift).astype(jnp.bfloat16)
    low1 = (matmul(normed1, adapt_qkv_in) * own_mask).astype(jnp.bfloat16)
    normed1_all, low1_small = (
        lax.all_gather(normed1, "tensor", axis=0, tiled=True),
        lax.all_gather(low1, "tensor", axis=0, tiled=True),
    )
    low1_all = low1_small
    qkv_arr = project_qkv(normed1_all, low1_all)
    qkv_seq = jnp.take(qkv_arr, order_row, axis=0)
    attended_seq, log_totals = attention_forward(qkv_seq, lengths_row, seq_len)
    attended = jnp.take(attended_seq.astype(jnp.bfloat16), inverse, axis=0)
    rows = attended
    mask_rows = group_mask
    part = matmul(rows, proj_joined)
    summed_attn = lax.psum_scatter(
        jnp.concatenate([part[:, :D], part[:, D:] * mask_rows], 1).astype(jnp.bfloat16),
        "tensor",
        scatter_dimension=0,
        tiled=True,
    ).astype(jnp.float32)
    proj_low = summed_attn[:, D:].astype(jnp.bfloat16)
    mid = inputs + summed_attn[:, :D] + matmul(proj_low, adapt_proj_out) + proj_bias
    normed2 = layer_norm(mid, norm2_gain, norm2_shift).astype(jnp.bfloat16)
    low2 = (matmul(normed2, adapt_up_in) * own_mask).astype(jnp.bfloat16)
    normed2_all, low2_small = (
        lax.all_gather(normed2, "tensor", axis=0, tiled=True),
        lax.all_gather(low2, "tensor", axis=0, tiled=True),
    )
    low2_all = low2_small
    upper = project_up(normed2_all, low2_all)
    active = gelu_tanh(upper).astype(jnp.bfloat16)
    rows = active
    mask_rows = group_mask
    part = matmul(rows, down_joined)
    summed_mlp = lax.psum_scatter(
        jnp.concatenate([part[:, :D], part[:, D:] * mask_rows], 1).astype(jnp.bfloat16),
        "tensor",
        scatter_dimension=0,
        tiled=True,
    ).astype(jnp.float32)
    down_low = summed_mlp[:, D:].astype(jnp.bfloat16)
    result = mid + summed_mlp[:, :D] + matmul(down_low, adapt_down_out) + down_bias
    grad_mlp = cotangent.astype(jnp.bfloat16)
    grad_down_low = (matmul_back(grad_mlp, adapt_down_out) * own_mask).astype(jnp.bfloat16)
    grad_down_out_part = matmul_over(down_low, grad_mlp)
    grad_mlp_all, grad_down_small = (
        lax.all_gather(grad_mlp, "tensor", axis=0, tiled=True),
        lax.all_gather(grad_down_low, "tensor", axis=0, tiled=True),
    )
    normed2_again, low2_again_small = (
        lax.all_gather(normed2, "tensor", axis=0, tiled=True),
        lax.all_gather(low2, "tensor", axis=0, tiled=True),
    )
    upper = project_up(normed2_again, low2_again_small)
    active = gelu_tanh(upper).astype(jnp.bfloat16)
    low2_all = low2_again_small
    grad_active = matmul_back(grad_mlp_all, down_weight) + matmul_back(
        grad_down_small, adapt_down_in
    )
    grad_down_in_part = matmul_over(active, grad_down_small)
    gelu_value, gelu_pull = jax.vjp(gelu_tanh, upper)
    grad_upper = gelu_pull(grad_active)[0].astype(jnp.bfloat16)
    grad_up_out_part = matmul_over(low2_all, grad_upper)
    rows = grad_upper
    part = matmul_back(rows, up_joined)
    summed_up = lax.psum_scatter(
        jnp.concatenate([part[:, :D], part[:, D:]], 1).astype(jnp.bfloat16),
        "tensor",
        scatter_dimension=0,
        tiled=True,
    ).astype(jnp.float32)
    grad_low2 = (summed_up[:, D:] * own_mask).astype(jnp.bfloat16)
    grad_up_in_part = matmul_over(normed2, grad_low2)
    grad_normed2 = summed_up[:, :D] + matmul_back(grad_low2, adapt_up_in)
    norm2_value, norm2_pull = jax.vjp(
        lambda values: layer_norm(values, norm2_gain, norm2_shift), mid
    )
    grad_mid = cotangent + norm2_pull(grad_normed2)[0]
    grad_attn = grad_mid.astype(jnp.bfloat16)
    grad_proj_low = (matmul_back(grad_attn, adapt_proj_out) * own_mask).astype(jnp.bfloat16)
    grad_proj_out_part = matmul_over(proj_low, grad_attn)
    grad_attn_all, grad_proj_small = (
        lax.all_gather(grad_attn, "tensor", axis=0, tiled=True),
        lax.all_gather(grad_proj_low, "tensor", axis=0, tiled=True),
    )
    grad_attended = matmul_back(grad_attn_all, proj_weight) + matmul_back(
        grad_proj_small, adapt_proj_in
    )
    grad_proj_in_part = matmul_over(attended, grad_proj_small)
    grad_attended_seq = jnp.take(grad_attended, order_row, axis=0).astype(jnp.bfloat16)
    normed1_again, low1_again_small = (
        lax.all_gather(normed1, "tensor", axis=0, tiled=True),
        lax.all_gather(low1, "tensor", axis=0, tiled=True),
    )
    qkv_seq = jnp.take(project_qkv(normed1_again, low1_again_small), order_row, axis=0)
    low1_all = low1_again_small
    grad_qkv_seq = attention_backward(qkv_seq, grad_attended_seq, log_totals, lengths_row, seq_len)
    grad_qkv = jnp.take(grad_qkv_seq.astype(jnp.bfloat16), inverse, axis=0)
    grad_qkv_out_part = jnp.einsum(
        "ra,rkc->akc", low1_all, grad_qkv, preferred_element_type=jnp.float32
    )
    rows = grad_qkv
    part = jnp.einsum("rkc,dkc->rd", rows, qkv_joined, preferred_element_type=jnp.float32)
    summed_qkv = lax.psum_scatter(
        jnp.concatenate([part[:, :D], part[:, D:]], 1).astype(jnp.bfloat16),
        "tensor",
        scatter_dimension=0,
        tiled=True,
    ).astype(jnp.float32)
    grad_low1 = (summed_qkv[:, D:] * own_mask).astype(jnp.bfloat16)
    grad_qkv_in_part = matmul_over(normed1, grad_low1)
    grad_normed1 = summed_qkv[:, :D] + matmul_back(grad_low1, adapt_qkv_in)
    norm1_value, norm1_pull = jax.vjp(
        lambda values: layer_norm(values, norm1_gain, norm1_shift), inputs
    )
    grad_input = grad_mid + norm1_pull(grad_normed1)[0]
    wide = lax.psum(
        (grad_qkv_in_part, grad_proj_out_part, grad_up_in_part, grad_down_out_part),
        ("dp", "tensor"),
    )
    narrow = (
        lax.psum(grad_qkv_out_part.astype(jnp.bfloat16), "dp").astype(jnp.float32),
        lax.psum(grad_proj_in_part.astype(jnp.bfloat16), "dp").astype(jnp.float32),
        lax.psum(grad_up_out_part.astype(jnp.bfloat16), "dp").astype(jnp.float32),
        lax.psum(grad_down_in_part.astype(jnp.bfloat16), "dp").astype(jnp.float32),
    )
    return (
        result,
        grad_input,
        wide[0],
        narrow[0],
        narrow[1],
        wide[1],
        wide[2],
        narrow[2],
        narrow[3],
        wide[3],
    )


def solution(mesh):
    in_specs = (
        P(("dp", "tensor"), None),
        P(("dp", "tensor"), None),
        P("dp", None),
        P("dp", None),
        P("dp", None),
        P(),
        P(),
        P(None, None, "tensor"),
        P(None, "tensor"),
        P("tensor", None),
        P(),
        P(),
        P(),
        P(None, "tensor"),
        P("tensor"),
        P("tensor", None),
        P(),
        P(),
        P(None, None, "tensor"),
        P("tensor", None),
        P(),
        P(),
        P(None, "tensor"),
        P("tensor", None),
        P(),
    )
    out_specs = (
        P(("dp", "tensor"), None),
        P(("dp", "tensor"), None),
        P(),
        P(None, None, "tensor"),
        P("tensor", None),
        P(),
        P(),
        P(None, "tensor"),
        P("tensor", None),
        P(),
    )
    return jax.shard_map(body, mesh=mesh, in_specs=in_specs, out_specs=out_specs, check_vma=False)
```

profile of v0, /device:TPU:0, one launch (start us, length us, event | category | flops | bytes accessed | tf_op | source)
XLA Modules:
  0.0 638.7 jit_solution(10005724395536461428)
XLA Ops:
  9.8 2.1 fusion.106
  12.8 4.3 scatter_custom_fusion
  20.2 8.9 %all_gather.29 = bf16[1024,128]{1,0:T(8,128)(2,1)S(1)} all-gather(bf16[256,128]{1,0:T(8,128)(2,1)S(1)} %fusion.97), channel_id=1, replica_groups=mesh['dp'=8,'tensor'=4] {'tensor'}, dimensions={0}, use_global_device_ids=true | all-gather | bytes 327680 | tf_op jit(solution)/shard_map/all_gather | solution.py:197
  31.9 6.9 %all-gather.5.cloned.1.call-done = bf16[1024,1024]{1,0:T(8,128)(2,1)} async-done(((bf16[256,1024]{1,0:T(8,128)(2,1)}), bf16[1024,1024]{1,0:T(8,128)(2,1)}) %all-gather.5.cloned.1.call-update) | async-done | bytes 2097168 | tf_op jit(solution)/shard_map/all_gather | solution.py:196
  38.8 3.8 fusion.84
  43.3 2.7 copy.65
  46.0 10.1 %gather_fusion.2 = bf16[1024,3,256]{2,1,0:T(4,128)(2,1)} fusion(bf16[1024,3,256]{2,1,0:T(4,128)(2,1)} %copy.65, s32[1024]{0:T(1024)S(1)} %fusion.129), kind=kCustom, calls=%fused_computation.clone | custom fusion | bytes 3149824 | tf_op jit(solution)/shard_map/jit(_take)/gather | solution.py:201
  56.1 6.3 broadcast_select_fusion.1
  62.4 2.9 copy.66
  65.3 15.9 %while.32 = (s32[]{:T(128)}, bf16[2,512,256]{1,2,0:T(8,128)(2,1)S(1)}, f32[2,4,512]{2,1,0:T(4,128)S(1)}, bf16[1024,3,4,64]{0,3,2,1:T(8,128)(2,1)S(1)}, s32[2]{0:...) while((s32[]{:T(128)}, ...), condition=%wide.region_7.9_spmd, body=%wide.region_4.8_spmd.sunk | while | flops 281541120 | bytes 18417900 | solution.py:72
  81.4 4.4 gather_fusion
  85.9 1.8 fusion.108
  91.6 32.2 %reduce-scatter.5.cloned.1.call-done = bf16[256,1152]{1,0:T(8,128)(2,1)} async-done(((bf16[1024,1152]{1,0:T(8,128)(2,1)}), bf16[256,1152]{1,0:T(8,128)(2,1)}) %reduce-scatter.5.cloned.1.call-update) | async-done | bytes 589840 | tf_op jit(solution)/shard_map/reduce_scatter | solution.py:207
  125.7 1.7 add_convert_fusion.1
  129.0 6.4 %all_gather.33 = bf16[1024,128]{1,0:T(8,128)(2,1)} all-gather(bf16[256,128]{1,0:T(8,128)(2,1)S(1)} %fusion.99), channel_id=1, replica_groups=mesh['dp'=8,'tensor'=4] {'tensor'}, dimensions={0}, use_global_device_ids=true | all-gather | bytes 327680 | tf_op jit(solution)/shard_map/all_gather | solution.py:240
  135.4 13.3 %all-gather.9.cloned.1.call-done = bf16[1024,1024]{1,0:T(8,128)(2,1)} async-done(((bf16[256,1024]{1,0:T(8,128)(2,1)}), bf16[1024,1024]{1,0:T(8,128)(2,1)}) %all-gather.9.cloned.1.call-update) | async-done | bytes 2097168 | tf_op jit(solution)/shard_map/all_gather | solution.py:239
  148.7 6.6 %fusion.153 = f32[1024,1024]{1,0:T(8,128)} fusion(bf16[1024,1024]{1,0:T(8,128)(2,1)} %all-gather.9.cloned.1.call-done, bf16[1024,1024]{1,0:T(8,128)(2,1)} %param.46), kind=kOutput, calls=%fused_computation.219 | convolution fusion | flops 2147483648 | bytes 8388608 | tf_op jit(solution)/shard_map/dot_general | solution.py:25
  155.6 5.8 all_gather.31
  161.4 12.0 %all-gather.7.cloned.1.call-done = bf16[1024,1024]{1,0:T(8,128)(2,1)} async-done(((bf16[256,1024]{1,0:T(8,128)(2,1)}), bf16[1024,1024]{1,0:T(8,128)(2,1)}) %all-gather.7.cloned.1.call-update) | async-done | bytes 2097168 | tf_op jit(solution)/shard_map/all_gather | solution.py:218
  173.4 4.6 fusion.152
  178.7 2.1 copy-done.18
  181.8 3.2 fusion.76
  186.5 4.2 convolution_convert_fusion
  190.7 33.2 %reduce-scatter.9.cloned.1.call-done = bf16[256,1152]{1,0:T(8,128)(2,1)} async-done(((bf16[1024,1152]{1,0:T(8,128)(2,1)}), bf16[256,1152]{1,0:T(8,128)(2,1)}) %reduce-scatter.9.cloned.1.call-update) | async-done | bytes 589840 | tf_op jit(solution)/shard_map/reduce_scatter | solution.py:258
  229.6 6.5 %fusion.77 = bf16[1024,1152]{1,0:T(8,128)(2,1)S(1)} fusion(bf16[1024,128]{1,0:T(8,128)(2,1)S(1)} %copy-done.64, bf16[1024,1024]{1,0:T(8,128)(2,1)} %param.46, f32[1024,1024]{1,0:T(8,128)} %copy-done.18), kind=kOutput, calls=%fused_computation.87 | convolution fusion | flops 2430074880 | bytes 8912896 | tf_op jit(solution)/shard_map/dot_general | solution.py:21
  240.9 4.8 convolution_convert_fusion.1
  246.1 6.3 all_gather.35
  252.3 2.2 convolution_convert_fusion.4
  254.6 2.4 fusion.154
  257.4 5.5 gather_fusion.1
  262.9 2.1 copy.68
  266.1 62.1 %while.33 = (s32[]{:T(128)}, bf16[2,512,4,64]{1,3,2,0:T(8,128)(2,1)}, bf16[2,512,4,64]{1,3,2,0:T(8,128)(2,1)}, bf16[2,512,4,64]{1,3,2,0:T(8,128)(2,1)}, bf16[102...) while((s32[]{:T(128)}, ...), condition=%wide.region_17.19_spmd, body=%wide.region_15.18_spmd.sunk | while | flops 686298624 | bytes 57437636 | solution.py:112
  271.6 2.8 fusion.230
  274.4 3.3 subtract_exponential_fusion.3
  277.6 7.9 %fusion.232 = bf16[2,512,4,64]{1,3,2,0:T(8,128)(2,1)} fusion(bf16[2,512,4,64]{1,3,2,0:T(8,128)(2,1)} %get-tuple-element.493, s32[]{:T(128)S(6)} %copy.112, f32[4,512,512]{1,2,0:T(8,128)} %subtract_exponential_fusion.3, f32[4,512,512]{1,2,0:T(8,128)} %fusion.230, bf16[1024,1,4,64]{0,3,2,1:T(8,128)(2,1)} %copy-done.5, s32[]{:T(128)S(6)} %select_n.203), kind=kOutput, calls=%fused_computation.43.clone.1 | convolution fusion | flops 139463168 | bytes 17563656 | tf_op jit(solution)/shard_map/while/body/eval_jaxpr/hqk,qhc->khc/dot_general | solution.py:102
  285.6 8.0 %fusion.231 = bf16[2,512,4,64]{1,3,2,0:T(8,128)(2,1)} fusion(bf16[2,512,4,64]{1,3,2,0:T(8,128)(2,1)} %get-tuple-element.492, s32[]{:T(128)S(6)} %copy.112, f32[4,512,512]{1,2,0:T(8,128)} %subtract_exponential_fusion.3, f32[4,512,512]{1,2,0:T(8,128)} %fusion.230, bf16[1024,1,4,64]{0,3,2,1:T(8,128)(2,1)} %copy-done.4, s32[]{:T(128)S(6)} %select_n.203), kind=kOutput, calls=%fused_computation.41.clone.1 | convolution fusion | flops 139463168 | bytes 17563656 | tf_op jit(solution)/shard_map/while/body/eval_jaxpr/hqk,khc->qhc/dot_general | solution.py:101
  293.6 3.7 fusion.233
  302.7 2.8 fusion.230
  305.4 3.3 subtract_exponential_fusion.3
  308.7 7.9 %fusion.232 = bf16[2,512,4,64]{1,3,2,0:T(8,128)(2,1)} fusion(bf16[2,512,4,64]{1,3,2,0:T(8,128)(2,1)} %get-tuple-element.493, s32[]{:T(128)S(6)} %copy.112, f32[4,512,512]{1,2,0:T(8,128)} %subtract_exponential_fusion.3, f32[4,512,512]{1,2,0:T(8,128)} %fusion.230, bf16[1024,1,4,64]{0,3,2,1:T(8,128)(2,1)} %copy-done.5, s32[]{:T(128)S(6)} %select_n.203), kind=kOutput, calls=%fused_computation.43.clone.1 | convolution fusion | flops 139463168 | bytes 17563656 | tf_op jit(solution)/shard_map/while/body/eval_jaxpr/hqk,qhc->khc/dot_general | solution.py:102
  316.6 8.0 %fusion.231 = bf16[2,512,4,64]{1,3,2,0:T(8,128)(2,1)} fusion(bf16[2,512,4,64]{1,3,2,0:T(8,128)(2,1)} %get-tuple-element.492, s32[]{:T(128)S(6)} %copy.112, f32[4,512,512]{1,2,0:T(8,128)} %subtract_exponential_fusion.3, f32[4,512,512]{1,2,0:T(8,128)} %fusion.230, bf16[1024,1,4,64]{0,3,2,1:T(8,128)(2,1)} %copy-done.4, s32[]{:T(128)S(6)} %select_n.203), kind=kOutput, calls=%fused_computation.41.clone.1 | convolution fusion | flops 139463168 | bytes 17563656 | tf_op jit(solution)/shard_map/while/body/eval_jaxpr/hqk,khc->qhc/dot_general | solution.py:101
  324.6 3.7 fusion.233
  328.3 2.4 copy.85
  330.6 3.9 reshape.388
  334.5 2.3 copy.83
  336.9 4.8 reshape.386
  343.0 4.8 reshape.387
  347.8 5.8 pad_maximum_fusion.2
  353.6 10.2 %gather_fusion.3 = bf16[1024,3,256]{2,1,0:T(4,128)(2,1)} fusion(bf16[1024,3,256]{2,1,0:T(4,128)(2,1)} %pad_maximum_fusion.2, s32[1024]{0:T(1024)S(1)} %copy-done.40), kind=kCustom, calls=%fused_computation.1.clone | custom fusion | bytes 3149824 | tf_op jit(solution)/shard_map/jit(_take)/gather | solution.py:290
  363.8 5.3 broadcast_select_fusion
  371.9 5.7 bitcast_convert_fusion
  377.7 1.9 fusion.122
  379.6 1.9 fusion.119
  381.6 2.0 fusion.132
  383.6 2.3 fusion.95
  386.0 61.0 %all-reduce.7.cloned.1.call-done = (bf16[128,3,256]{2,0,1:T(8,128)(2,1)}, bf16[256,128]{1,0:T(8,128)(2,1)}, bf16[128,1024]{1,0:T(8,128)(2,1)}, bf16[1024,128]{1,0:T(8,128)(2,1)}) async-done(((bf16[128,3,256]{2,0,1:T(8,128)(2,1)}, bf16[256,128]{1,0:T(8,128)(2,1)}, bf16[128,1024]{1,0:T(8,128)(2,1)}, bf16[1024,128]{1,0:T(8,128)(2,1)}), (bf16[128,3,256]{2,0,1:T(8,128)(2,1)}, bf16[256,128]{1,0:T(8,128)(2,1)}, ...) | async-done | bytes 786448 | tf_op jit(solution)/shard_map/psum | solution.py:314
  450.2 1.8 convert_element_type.148
  451.9 1.8 convert_element_type.150
  453.7 27.9 %reduce-scatter.11.cloned.1.call-done = bf16[256,1152]{1,0:T(8,128)(2,1)} async-done(((bf16[1024,1152]{1,0:T(8,128)(2,1)}), bf16[256,1152]{1,0:T(8,128)(2,1)}) %reduce-scatter.11.cloned.1.call-update) | async-done | bytes 589840 | tf_op jit(solution)/shard_map/reduce_scatter | solution.py:296
  489.3 134.8 %all-reduce.5.cloned.1.call-done = (f32[1024,128]{1,0:T(8,128)}, f32[128,1024]{1,0:T(8,128)}, f32[1024,128]{1,0:T(8,128)}, f32[128,1024]{1,0:T(8,128)}) async-done(((f32[1024,128]{1,0:T(8,128)}, f32[128,1024]{1,0:T(8,128)}, f32[1024,128]{1,0:T(8,128)}, f32[128,1024]{1,0:T(8,128)}), (f32[1024,128]{1,0:T(8,128)}, f32[128,1024]{1,0:T(8,128)}, f32[1024,128]{1,0:T(8,128)}, ...) | async-done | bytes 2097168 | tf_op jit(solution)/shard_map/psum | solution.py:309
  624.1 1.9 copy.137
  626.0 1.9 copy.138
  627.9 1.9 copy.139
  629.7 1.9 copy.140
  (261 shorter events, 63.9 us)
Async XLA Ops:
  7.2 148.1 %copy-start = (bf16[1024,128]{1,0:T(8,128)(2,1)S(1)}, bf16[1024,128]{1,0:T(8,128)(2,1)}, u32[]{:S(2)}) copy-start(bf16[1024,128]{1,0:T(8,128)(2,1)} %param.52) | copy-start | bytes 786436
  7.2 31.6 %all-gather.5.cloned.1.call-start = ((), (), s32[]{:S(2)}) async-start(), calls=%async_computation.4 | async-start | bytes 2621440 | tf_op jit(solution)/shard_map/all_gather | solution.py:196
  8.5 30.4 %copy-start.38 = (f32[256]{0:T(256)}, f32[256]{0:T(256)S(1)}, u32[]{:S(2)}) copy-start(f32[256]{0:T(256)S(1)} %broadcast_multiply_fusion.1) | copy-start | bytes 3076
  9.8 29.0 %copy-start.55 = (f32[256]{0:T(256)}, f32[256]{0:T(256)S(1)}, u32[]{:S(2)}) copy-start(f32[256]{0:T(256)S(1)} %fusion.103) | copy-start | bytes 3076
  9.8 29.0 %copy-start.46 = (f32[256]{0:T(256)}, f32[256]{0:T(256)S(1)}, u32[]{:S(2)}) copy-start(f32[256]{0:T(256)S(1)} %fusion.138) | copy-start | bytes 3076
  12.0 111.8 %reduce-scatter.5.cloned.1.call-start = ((), (), s32[]{:S(2)}) async-start(), calls=%async_computation.5 | async-start | bytes 2949120 | tf_op jit(solution)/shard_map/reduce_scatter | solution.py:207
  12.8 4.3 copy-start.44
  17.2 14.0 %copy-start.58 = (s32[128]{0:T(128)}, s32[128]{0:T(128)S(1)}, u32[]{:S(2)}) copy-start(s32[128]{0:T(128)S(1)} %and_select_fusion) | copy-start | bytes 1540
  18.5 24.1 %copy-start.36 = (s32[1024]{0:T(1024)}, s32[1024]{0:T(1024)S(1)}, u32[]{:S(2)}) copy-start(s32[1024]{0:T(1024)S(1)} %fusion.125) | copy-start | bytes 12292
  29.1 13.6 %copy-start.19 = (bf16[1024,128]{1,0:T(8,128)(2,1)}, bf16[1024,128]{1,0:T(8,128)(2,1)S(1)}, u32[]{:S(2)}) copy-start(bf16[1024,128]{1,0:T(8,128)(2,1)S(1)} %all_gather.29) | copy-start | bytes 786436
  31.2 24.9 %copy-start.49 = (pred[1024]{0:T(1024)(128)(4,1)}, pred[1024]{0:T(1024)(128)(4,1)S(1)}, u32[]{:S(2)}) copy-start(pred[1024]{0:T(1024)(128)(4,1)S(1)} %compare_and_fusion) | copy-start | bytes 3076
  31.9 10.8 %copy-start.34 = (bf16[128,3,256]{2,0,1:T(8,128)(2,1)S(1)}, bf16[128,3,256]{2,0,1:T(8,128)(2,1)}, u32[]{:S(2)}) copy-start(bf16[128,3,256]{2,0,1:T(8,128)(2,1)} %param.49) | copy-start | bytes 589828
  56.1 9.2 %copy-start.65 = (s32[1,2]{1,0:T(1,128)S(1)}, s32[1,2]{1,0:T(1,128)}, u32[]{:S(2)}) copy-start(s32[1,2]{1,0:T(1,128)} %param.33) | copy-start | bytes 28
  81.2 4.7 copy-start.29
  88.9 34.9 %copy-start.2 = (bf16[256,1024]{1,0:T(8,128)(2,1)S(1)}, bf16[256,1024]{1,0:T(8,128)(2,1)}, u32[]{:S(2)}) copy-start(bf16[256,1024]{1,0:T(8,128)(2,1)} %param.31) | copy-start | bytes 1572868
  90.6 58.1 %all-gather.9.cloned.1.call-start = ((), (), s32[]{:S(2)}) async-start(), calls=%async_computation.8 | async-start | bytes 2621440 | tf_op jit(solution)/shard_map/all_gather | solution.py:239
  91.6 81.8 %all-gather.7.cloned.1.call-start = ((), (), s32[]{:S(2)}) async-start(), calls=%async_computation.6 | async-start | bytes 2621440 | tf_op jit(solution)/shard_map/all_gather | solution.py:218
  127.5 96.4 %reduce-scatter.9.cloned.1.call-start = ((), (), s32[]{:S(2)}) async-start(), calls=%async_computation.9 | async-start | bytes 2949120 | tf_op jit(solution)/shard_map/reduce_scatter | solution.py:258
  135.4 19.9 %copy-start.15 = (bf16[256,1024]{1,0:T(8,128)(2,1)S(1)}, bf16[256,1024]{1,0:T(8,128)(2,1)}, u32[]{:S(2)}) copy-start(bf16[256,1024]{1,0:T(8,128)(2,1)} %add_convert_fusion.1) | copy-start | bytes 1572868
  161.3 16.6 %copy-start.31 = (bf16[128,1024]{1,0:T(8,128)(2,1)S(1)}, bf16[128,1024]{1,0:T(8,128)(2,1)}, u32[]{:S(2)}) copy-start(bf16[128,1024]{1,0:T(8,128)(2,1)} %param.53) | copy-start | bytes 786436
  173.4 4.6 copy-start.60
  178.0 2.9 copy-start.32
  178.0 2.9 copy-start.63
  178.0 3.9 copy-start.68
  181.8 4.6 copy-start.62
  190.7 35.7 %copy-start.57 = (f32[256]{0:T(256)S(1)}, f32[256]{0:T(256)}, u32[]{:S(2)}) copy-start(f32[256]{0:T(256)} %copy-done.56) | copy-start | bytes 3076
  190.7 35.8 %copy-start.42 = (f32[256]{0:T(256)S(1)}, f32[256]{0:T(256)}, u32[]{:S(2)}) copy-start(f32[256]{0:T(256)} %copy-done.41) | copy-start | bytes 3076
  190.7 35.8 %copy-start.54 = (f32[256]{0:T(256)S(1)}, f32[256]{0:T(256)}, u32[]{:S(2)}) copy-start(f32[256]{0:T(256)} %copy-done.53) | copy-start | bytes 3076
  190.7 63.9 %all-gather.11.cloned.1.call-start = ((), (), s32[]{:S(2)}) async-start(), calls=%async_computation.10 | async-start | bytes 2621440 | tf_op jit(solution)/shard_map/all_gather | solution.py:275
  223.9 4.0 copy-start.7
  225.1 3.8 copy-start.45
  226.4 3.2 copy-start.64
  228.9 150.7 %reduce-scatter.7.cloned.1.call-start = ((), (), s32[]{:S(2)}) async-start(), calls=%async_computation.7 | async-start | bytes 2949120 | tf_op jit(solution)/shard_map/reduce_scatter | solution.py:227
  240.9 4.9 copy-start.12
  240.9 4.9 copy-start.26
  245.7 201.2 %all-reduce.7.cloned.1.call-start = ((), (), s32[]{:S(2)}) async-start(), calls=%async_computation.13 | async-start | bytes 1572864 | tf_op jit(solution)/shard_map/psum | solution.py:314
  257.3 7.6 %copy-start.50 = (pred[1024]{0:T(1024)(128)(4,1)S(1)}, pred[1024]{0:T(1024)(128)(4,1)}, u32[]{:S(2)}) copy-start(pred[1024]{0:T(1024)(128)(4,1)} %copy-done.49) | copy-start | bytes 3076
  266.1 5.1 copy-start.66
  285.6 11.7 %copy-start.67 = (s32[2]{0:T(128)S(1)}, s32[2]{0:T(128)}, u32[]{:S(2)}) copy-start(s32[2]{0:T(128)} %copy-done.66) | copy-start | bytes 28 | tf_op jit(solution)/shard_map/while
  297.2 5.1 copy-start.66
  302.6 2.8 copy-start.4
  316.6 11.7 %copy-start.67 = (s32[2]{0:T(128)S(1)}, s32[2]{0:T(128)}, u32[]{:S(2)}) copy-start(s32[2]{0:T(128)} %copy-done.66) | copy-start | bytes 28 | tf_op jit(solution)/shard_map/while
  328.3 13.4 %copy-start.30 = (bf16[2,512,4,64]{1,3,2,0:T(8,128)(2,1)S(1)}, bf16[2,512,4,64]{1,3,2,0:T(8,128)(2,1)}, u32[]{:S(2)}) copy-start(bf16[2,512,4,64]{1,3,2,0:T(8,128)(2,1)} %get-tuple-element.261) | copy-start | bytes 1572868
  341.6 12.0 %copy-start.40 = (s32[1024]{0:T(1024)S(1)}, s32[1024]{0:T(1024)}, u32[]{:S(2)}) copy-start(s32[1024]{0:T(1024)} %get-tuple-element.326) | copy-start | bytes 12292
  347.8 16.0 %copy-start.48 = (pred[1024]{0:T(1024)(128)(4,1)S(1)}, pred[1024]{0:T(1024)(128)(4,1)}, u32[]{:S(2)}) copy-start(pred[1024]{0:T(1024)(128)(4,1)} %compare_and_fusion.1) | copy-start | bytes 3076
  353.6 16.8 %copy-start.20 = (bf16[1024,128]{1,0:T(8,128)(2,1)S(1)}, bf16[1024,128]{1,0:T(8,128)(2,1)}, u32[]{:S(2)}) copy-start(bf16[1024,128]{1,0:T(8,128)(2,1)} %copy-done.19) | copy-start | bytes 786436
  363.8 8.1 %copy-start.35 = (bf16[128,3,256]{2,0,1:T(8,128)(2,1)S(1)}, bf16[128,3,256]{2,0,1:T(8,128)(2,1)}, u32[]{:S(2)}) copy-start(bf16[128,3,256]{2,0,1:T(8,128)(2,1)} %param.49) | copy-start | bytes 589828
  371.5 6.1 copy-start.13
  371.6 8.1 %copy-start.11 = (bf16[256,1024]{1,0:T(8,128)(2,1)S(1)}, bf16[256,1024]{1,0:T(8,128)(2,1)}, u32[]{:S(2)}) copy-start(bf16[256,1024]{1,0:T(8,128)(2,1)} %convert_element_type.131) | copy-start | bytes 1572868
  371.6 110.1 %reduce-scatter.11.cloned.1.call-start = ((), (), s32[]{:S(2)}) async-start(), calls=%async_computation.11 | async-start | bytes 2949120 | tf_op jit(solution)/shard_map/reduce_scatter | solution.py:296
  377.6 4.0 copy-start.16
  377.6 6.0 copy-start.27
  377.6 6.0 copy-start.61
  377.6 246.5 %all-reduce.5.cloned.1.call-start = ((), (), s32[]{:S(2)}) async-start(), calls=%async_computation.12 | async-start | bytes 4194304 | tf_op jit(solution)/shard_map/psum | solution.py:309
  379.6 104.2 %copy-start.14 = (bf16[256,1024]{1,0:T(8,128)(2,1)S(1)}, bf16[256,1024]{1,0:T(8,128)(2,1)}, u32[]{:S(2)}) copy-start(bf16[256,1024]{1,0:T(8,128)(2,1)} %fusion.106) | copy-start | bytes 1572868
  386.0 99.1 %copy-start.3 = (bf16[256,1024]{1,0:T(8,128)(2,1)S(1)}, bf16[256,1024]{1,0:T(8,128)(2,1)}, u32[]{:S(2)}) copy-start(bf16[256,1024]{1,0:T(8,128)(2,1)} %param.31) | copy-start | bytes 1572868
  386.0 99.1 %copy-start.28 = (bf16[1024,128]{1,0:T(8,128)(2,1)S(1)}, bf16[1024,128]{1,0:T(8,128)(2,1)}, u32[]{:S(2)}) copy-start(bf16[1024,128]{1,0:T(8,128)(2,1)} %param.48) | copy-start | bytes 786436
  386.0 99.1 %copy-start.39 = (f32[256]{0:T(256)S(1)}, f32[256]{0:T(256)}, u32[]{:S(2)}) copy-start(f32[256]{0:T(256)} %copy-done.38) | copy-start | bytes 3076
  386.0 99.1 %copy-start.43 = (f32[1024]{0:T(1024)S(1)}, f32[1024]{0:T(1024)}, u32[]{:S(2)}) copy-start(f32[1024]{0:T(1024)} %param.36) | copy-start | bytes 12292
  450.2 37.3 %copy-start.47 = (f32[256]{0:T(256)S(1)}, f32[256]{0:T(256)}, u32[]{:S(2)}) copy-start(f32[256]{0:T(256)} %copy-done.46) | copy-start | bytes 3076
  453.7 34.1 %copy-start.8 = (f32[256,1024]{1,0:T(8,128)S(1)}, f32[256,1024]{1,0:T(8,128)}, u32[]{:S(2)}) copy-start(f32[256,1024]{1,0:T(8,128)} %param.32) | copy-start | bytes 3145732
  453.7 34.1 %copy-start.10 = (f32[256,1024]{1,0:T(8,128)S(1)}, f32[256,1024]{1,0:T(8,128)}, u32[]{:S(2)}) copy-start(f32[256,1024]{1,0:T(8,128)} %copy-done.9) | copy-start | bytes 3145732
  453.7 34.1 %copy-start.52 = (f32[256]{0:T(256)S(1)}, f32[256]{0:T(256)}, u32[]{:S(2)}) copy-start(f32[256]{0:T(256)} %copy-done.51) | copy-start | bytes 3076
  487.8 143.8 %copy-start.1 = (bf16[1024,128]{1,0:T(8,128)(2,1)S(1)}, bf16[1024,128]{1,0:T(8,128)(2,1)}, u32[]{:S(2)}) copy-start(bf16[1024,128]{1,0:T(8,128)(2,1)} %param.52) | copy-start | bytes 786436
  (19 other events, 35.3 us)
Sparse Core Ops, SparseCore 0:
  12.1 26.6 all-gather.4
  90.7 33.0 reduce-scatter.4
  126.0 22.5 all-gather.8
  150.7 22.5 all-gather.6
  190.8 33.0 reduce-scatter.8
  229.0 23.5 all-gather.10
  255.1 33.1 reduce-scatter.6
  371.7 75.2 all-reduce.6
  449.5 32.0 reduce-scatter.10
  489.2 134.8 all-reduce.4
where the time goes:
time: 643 us; the launch traced here: 639 us
  waiting for transfers between devices  321 us (50%)
  matrix products  123 us (19%)
  local copies, waits for them, and re-layouts  87.2 us (14%)
  other arithmetic  53.3 us (8%)
  blocking collectives  27.4 us (4%)
  between operations  15.3 us (2%)
  loops' own time  10.6 us (2%)
    psum x1, waiting for transfers between devices, body(): lax.psum((grad_qkv_in_part, grad_proj_out_part, grad_up_in_part, grad_dow...  135 us
    reduce_scatter x2, waiting for transfers between devices, body(): lax.psum_scatter(jnp.concatenate([part[:, :D], part[:, D:]], 1).astype(jn...  61 us
    psum x1, waiting for transfers between devices, body(): lax.psum(grad_qkv_out_part.astype(jnp.bfloat16), 'dp').astype(jnp.float32)  61 us
    reduce_scatter x2, waiting for transfers between devices, body(): lax.psum_scatter(jnp.concatenate([part[:, :D], part[:, D:] * mask_rows],...  32.2 us
    dot_general x9, matrix products, matmul_back(): lax.dot_general(left, right, (((1,), (1,)), ((), ())), preferred_element_...  21.5 us
    another operation x6, local copies, waits for them, and re-layouts, attention_backward(): return jnp.stack([grad_query, grad_key, grad_value], 1)  19.6 us
    dot_general x8, matrix products, matmul(): return jnp.dot(left, right, preferred_element_type=jnp.float32)  19.2 us
    unnamed x134, local copies, waits for them, and re-layouts  17.1 us
  transfers between devices with their start and end apart: 10, of which 8 were waited for; matrix products, arithmetic and copies ran while one was open for 28% of the time, Pallas kernels for 0%

commit v1 on v0

--- a/solution.py
+++ b/solution.py
@@ -1,3 +1,4 @@
+import functools
 import math
 import jax
 import jax.numpy as jnp
@@ -9,6 +10,14 @@
 RANK = 16
 EPSILON = 1e-05
 NEGATIVE = -1000000000.0
+
+
+def set_stacks_all(vector, axis_tag):
+    everything = jnp.sum(lax.all_gather(vector, axis_name=axis_tag), axis=0)
+    return everything
+
+
+pack_teams = functools.partial(set_stacks_all, axis_tag="dp")
 
 
 def layer_norm(values, gain, shift):
@@ -311,7 +320,7 @@
         ("dp", "tensor"),
     )
     narrow = (
-        lax.psum(grad_qkv_out_part.astype(jnp.bfloat16), "dp").astype(jnp.float32),
+        pack_teams(grad_qkv_out_part.astype(jnp.bfloat16)).astype(jnp.float32),
         lax.psum(grad_proj_in_part.astype(jnp.bfloat16), "dp").astype(jnp.float32),
         lax.psum(grad_up_out_part.astype(jnp.bfloat16), "dp").astype(jnp.float32),
         lax.psum(grad_down_in_part.astype(jnp.bfloat16), "dp").astype(jnp.float32),

time: 643 us -> 612 us (0.952)
  waiting for transfers between devices: 321 us -> 289 us
    psum x1, waiting for transfers between devices: 61 us -> 0.01 us  [body(): lax.psum(grad_proj_in_part.astype(jnp.bfloat16), 'dp').astype(jnp.float32)]
    all_gather x0 -> x1, waiting for transfers between devices: none -> 24.8 us  [set_stacks_all(): everything = jnp.sum(lax.all_gather(vector, axis_name=axis_tag), axis=0)]
    unnamed x134 -> x132, local copies, waits for them, and re-layouts: 17.1 us -> 16 us
  transfers between devices with their start and end apart: 10 -> 11, of which waited for: 8 -> 8; matrix products, arithmetic and copies ran while one was open for 28% -> 29% of each run, Pallas kernels for 0% -> 0%
where the time goes in v1:
time: 612 us; the launch traced here: 607 us
  waiting for transfers between devices  289 us (47%)
  matrix products  124 us (20%)
  local copies, waits for them, and re-layouts  86.1 us (14%)
  other arithmetic  54.2 us (9%)
  blocking collectives  26.9 us (4%)
  between operations  15 us (2%)
  loops' own time  10.6 us (2%)
    psum x1, waiting for transfers between devices, body(): lax.psum((grad_qkv_in_part, grad_proj_out_part, grad_up_in_part, grad_dow...  135 us
    reduce_scatter x2, waiting for transfers between devices, body(): lax.psum_scatter(jnp.concatenate([part[:, :D], part[:, D:]], 1).astype(jn...  65 us
    reduce_scatter x2, waiting for transfers between devices, body(): lax.psum_scatter(jnp.concatenate([part[:, :D], part[:, D:] * mask_rows],...  32.2 us
    all_gather x1, waiting for transfers between devices, set_stacks_all(): everything = jnp.sum(lax.all_gather(vector, axis_name=axis_tag), axis=0)  24.8 us
    dot_general x9, matrix products, matmul_back(): lax.dot_general(left, right, (((1,), (1,)), ((), ())), preferred_element_...  22.2 us
    another operation x6, local copies, waits for them, and re-layouts, attention_backward(): return jnp.stack([grad_query, grad_key, grad_value], 1)  19.6 us
    dot_general x8, matrix products, matmul(): return jnp.dot(left, right, preferred_element_type=jnp.float32)  19.3 us
    dot_general x2, matrix products, one_block(): jnp.einsum('hqk,khc->qhc', grad_raw, keys, preferred_element_type=jnp.flo...  16 us
  transfers between devices with their start and end apart: 11, of which 8 were waited for; matrix products, arithmetic and copies ran while one was open for 29% of the time, Pallas kernels for 0%

profile of v1, /device:TPU:0, one launch (start us, length us, event | category | flops | bytes accessed | tf_op | source)
XLA Modules:
  0.0 607.1 jit_solution(16322936307228219762)
XLA Ops:
  9.8 2.1 fusion.106
  12.8 4.3 scatter_custom_fusion
  20.1 8.9 %all_gather.35 = bf16[1024,128]{1,0:T(8,128)(2,1)S(1)} all-gather(bf16[256,128]{1,0:T(8,128)(2,1)S(1)} %fusion.97), channel_id=1, replica_groups=mesh['dp'=8,'tensor'=4] {'tensor'}, dimensions={0}, use_global_device_ids=true | all-gather | bytes 327680 | tf_op jit(solution)/shard_map/all_gather | solution.py:206
  31.9 6.9 %all-gather.7.cloned.1.call-done = bf16[1024,1024]{1,0:T(8,128)(2,1)} async-done(((bf16[256,1024]{1,0:T(8,128)(2,1)}), bf16[1024,1024]{1,0:T(8,128)(2,1)}) %all-gather.7.cloned.1.call-update) | async-done | bytes 2097168 | tf_op jit(solution)/shard_map/all_gather | solution.py:205
  38.8 3.8 fusion.84
  43.3 2.8 copy.65
  46.0 10.1 %gather_fusion.2 = bf16[1024,3,256]{2,1,0:T(4,128)(2,1)} fusion(bf16[1024,3,256]{2,1,0:T(4,128)(2,1)} %copy.65, s32[1024]{0:T(1024)S(1)} %fusion.129), kind=kCustom, calls=%fused_computation.clone | custom fusion | bytes 3149824 | tf_op jit(solution)/shard_map/jit(_take)/gather | solution.py:210
  56.2 6.3 %broadcast_select_fusion.1 = bf16[1024,3,256]{2,1,0:T(4,128)(2,1)} fusion(bf16[1024,3,256]{2,1,0:T(4,128)(2,1)} %gather_fusion.2, pred[1024]{0:T(1024)(128)(4,1)S(1)} %compare_and_fusion), kind=kLoop, calls=%fused_computation.99 | loop fusion | flops 786432 | bytes 3146752 | tf_op jit(solution)/shard_map/jit(_take)/select_n | solution.py:210
  62.5 2.9 copy.66
  65.4 15.9 %while.32 = (s32[]{:T(128)}, bf16[2,512,256]{1,2,0:T(8,128)(2,1)S(1)}, f32[2,4,512]{2,1,0:T(4,128)S(1)}, bf16[1024,3,4,64]{0,3,2,1:T(8,128)(2,1)S(1)}, s32[2]{0:...) while((s32[]{:T(128)}, ...), condition=%wide.region_7.9_spmd, body=%wide.region_4.8_spmd.sunk | while | flops 281541120 | bytes 18417900 | solution.py:81
  81.5 4.4 gather_fusion
  86.0 1.8 fusion.108
  91.8 32.2 %reduce-scatter.5.cloned.1.call-done = bf16[256,1152]{1,0:T(8,128)(2,1)} async-done(((bf16[1024,1152]{1,0:T(8,128)(2,1)}), bf16[256,1152]{1,0:T(8,128)(2,1)}) %reduce-scatter.5.cloned.1.call-update) | async-done | bytes 589840 | tf_op jit(solution)/shard_map/reduce_scatter | solution.py:216
  125.8 1.8 add_convert_fusion.1
  129.1 6.4 %all_gather.39 = bf16[1024,128]{1,0:T(8,128)(2,1)} all-gather(bf16[256,128]{1,0:T(8,128)(2,1)S(1)} %fusion.99), channel_id=1, replica_groups=mesh['dp'=8,'tensor'=4] {'tensor'}, dimensions={0}, use_global_device_ids=true | all-gather | bytes 327680 | tf_op jit(solution)/shard_map/all_gather | solution.py:249
  135.5 13.3 %all-gather.11.cloned.1.call-done = bf16[1024,1024]{1,0:T(8,128)(2,1)} async-done(((bf16[256,1024]{1,0:T(8,128)(2,1)}), bf16[1024,1024]{1,0:T(8,128)(2,1)}) %all-gather.11.cloned.1.call-update) | async-done | bytes 2097168 | tf_op jit(solution)/shard_map/all_gather | solution.py:248
  148.8 6.5 %fusion.153 = f32[1024,1024]{1,0:T(8,128)} fusion(bf16[1024,1024]{1,0:T(8,128)(2,1)} %all-gather.11.cloned.1.call-done, bf16[1024,1024]{1,0:T(8,128)(2,1)} %param.46), kind=kOutput, calls=%fused_computation.219 | convolution fusion | flops 2147483648 | bytes 8388608 | tf_op jit(solution)/shard_map/dot_general | solution.py:34
  155.6 5.8 all_gather.37
  161.4 12.1 %all-gather.9.cloned.1.call-done = bf16[1024,1024]{1,0:T(8,128)(2,1)} async-done(((bf16[256,1024]{1,0:T(8,128)(2,1)}), bf16[1024,1024]{1,0:T(8,128)(2,1)}) %all-gather.9.cloned.1.call-update) | async-done | bytes 2097168 | tf_op jit(solution)/shard_map/all_gather | solution.py:227
  173.5 4.6 fusion.152
  178.8 2.1 copy-done.18
  182.0 3.2 fusion.76
  186.5 4.2 convolution_convert_fusion
  190.8 33.1 %reduce-scatter.9.cloned.1.call-done = bf16[256,1152]{1,0:T(8,128)(2,1)} async-done(((bf16[1024,1152]{1,0:T(8,128)(2,1)}), bf16[256,1152]{1,0:T(8,128)(2,1)}) %reduce-scatter.9.cloned.1.call-update) | async-done | bytes 589840 | tf_op jit(solution)/shard_map/reduce_scatter | solution.py:267
  228.9 6.6 %fusion.77 = bf16[1024,1152]{1,0:T(8,128)(2,1)S(1)} fusion(bf16[1024,128]{1,0:T(8,128)(2,1)} %param.54, bf16[1024,1024]{1,0:T(8,128)(2,1)} %param.46, f32[1024,1024]{1,0:T(8,128)} %copy-done.18), kind=kOutput, calls=%fused_computation.87 | convolution fusion | flops 2430074880 | bytes 8912896 | tf_op jit(solution)/shard_map/dot_general | solution.py:30
  238.8 2.8 convolution_convert_fusion.2
  241.6 4.8 convolution_convert_fusion.1
  246.7 5.8 all_gather.41
  253.8 2.4 fusion.154
  257.4 5.5 gather_fusion.1
  262.9 2.1 copy.68
  266.1 61.9 %while.33 = (s32[]{:T(128)}, bf16[2,512,4,64]{1,3,2,0:T(8,128)(2,1)}, bf16[2,512,4,64]{1,3,2,0:T(8,128)(2,1)}, bf16[2,512,4,64]{1,3,2,0:T(8,128)(2,1)}, bf16[102...) while((s32[]{:T(128)}, ...), condition=%wide.region_17.19_spmd, body=%wide.region_15.18_spmd.sunk | while | flops 686298624 | bytes 57437636 | solution.py:121
  271.6 2.7 fusion.230
  274.3 3.2 subtract_exponential_fusion.3
  277.5 7.9 %fusion.232 = bf16[2,512,4,64]{1,3,2,0:T(8,128)(2,1)} fusion(bf16[2,512,4,64]{1,3,2,0:T(8,128)(2,1)} %get-tuple-element.492, s32[]{:T(128)S(6)} %copy.112, f32[4,512,512]{1,2,0:T(8,128)} %subtract_exponential_fusion.3, f32[4,512,512]{1,2,0:T(8,128)} %fusion.230, bf16[1024,1,4,64]{0,3,2,1:T(8,128)(2,1)} %copy-done.5, s32[]{:T(128)S(6)} %select_n.203), kind=kOutput, calls=%fused_computation.43.clone.1 | convolution fusion | flops 139463168 | bytes 17563656 | tf_op jit(solution)/shard_map/while/body/eval_jaxpr/hqk,qhc->khc/dot_general | solution.py:111
  285.5 8.0 %fusion.231 = bf16[2,512,4,64]{1,3,2,0:T(8,128)(2,1)} fusion(bf16[2,512,4,64]{1,3,2,0:T(8,128)(2,1)} %get-tuple-element.491, s32[]{:T(128)S(6)} %copy.112, f32[4,512,512]{1,2,0:T(8,128)} %subtract_exponential_fusion.3, f32[4,512,512]{1,2,0:T(8,128)} %fusion.230, bf16[1024,1,4,64]{0,3,2,1:T(8,128)(2,1)} %copy-done.4, s32[]{:T(128)S(6)} %select_n.203), kind=kOutput, calls=%fused_computation.41.clone.1 | convolution fusion | flops 139463168 | bytes 17563656 | tf_op jit(solution)/shard_map/while/body/eval_jaxpr/hqk,khc->qhc/dot_general | solution.py:110
  293.5 3.7 fusion.233
  302.6 2.7 fusion.230
  305.3 3.3 subtract_exponential_fusion.3
  308.5 7.9 %fusion.232 = bf16[2,512,4,64]{1,3,2,0:T(8,128)(2,1)} fusion(bf16[2,512,4,64]{1,3,2,0:T(8,128)(2,1)} %get-tuple-element.492, s32[]{:T(128)S(6)} %copy.112, f32[4,512,512]{1,2,0:T(8,128)} %subtract_exponential_fusion.3, f32[4,512,512]{1,2,0:T(8,128)} %fusion.230, bf16[1024,1,4,64]{0,3,2,1:T(8,128)(2,1)} %copy-done.5, s32[]{:T(128)S(6)} %select_n.203), kind=kOutput, calls=%fused_computation.43.clone.1 | convolution fusion | flops 139463168 | bytes 17563656 | tf_op jit(solution)/shard_map/while/body/eval_jaxpr/hqk,qhc->khc/dot_general | solution.py:111
  316.4 8.0 %fusion.231 = bf16[2,512,4,64]{1,3,2,0:T(8,128)(2,1)} fusion(bf16[2,512,4,64]{1,3,2,0:T(8,128)(2,1)} %get-tuple-element.491, s32[]{:T(128)S(6)} %copy.112, f32[4,512,512]{1,2,0:T(8,128)} %subtract_exponential_fusion.3, f32[4,512,512]{1,2,0:T(8,128)} %fusion.230, bf16[1024,1,4,64]{0,3,2,1:T(8,128)(2,1)} %copy-done.4, s32[]{:T(128)S(6)} %select_n.203), kind=kOutput, calls=%fused_computation.41.clone.1 | convolution fusion | flops 139463168 | bytes 17563656 | tf_op jit(solution)/shard_map/while/body/eval_jaxpr/hqk,khc->qhc/dot_general | solution.py:110
  324.4 3.7 fusion.233
  328.0 2.4 copy.85
  330.4 3.9 reshape.389
  334.3 2.3 copy.83
  336.6 4.8 reshape.387
  342.8 4.8 reshape.388
  347.6 5.8 pad_maximum_fusion.2
  353.4 10.2 %gather_fusion.3 = bf16[1024,3,256]{2,1,0:T(4,128)(2,1)} fusion(bf16[1024,3,256]{2,1,0:T(4,128)(2,1)} %pad_maximum_fusion.2, s32[1024]{0:T(1024)S(1)} %copy-done.39), kind=kCustom, calls=%fused_computation.1.clone | custom fusion | bytes 3149824 | tf_op jit(solution)/shard_map/jit(_take)/gather | solution.py:299
  363.6 5.3 broadcast_select_fusion
  371.7 5.7 bitcast_convert_fusion
  377.6 1.9 fusion.122
  379.5 1.9 fusion.119
  381.4 2.0 fusion.132
  383.5 2.4 fusion.95
  387.4 1.8 convert_element_type.150
  389.2 1.9 convert_element_type.152
  391.0 24.8 %all-gather.15.cloned.1.call-done = bf16[1024,3,256]{2,0,1:T(8,128)(2,1)} async-done(((bf16[128,3,256]{2,0,1:T(8,128)(2,1)}), bf16[1024,3,256]{2,0,1:T(8,128)(2,1)}) %all-gather.15.cloned.1.call-update) | async-done | bytes 1572880 | tf_op jit(solution)/shard_map/all_gather | solution.py:16
  418.3 31.8 %reduce-scatter.11.cloned.1.call-done = bf16[256,1152]{1,0:T(8,128)(2,1)} async-done(((bf16[1024,1152]{1,0:T(8,128)(2,1)}), bf16[256,1152]{1,0:T(8,128)(2,1)}) %reduce-scatter.11.cloned.1.call-update) | async-done | bytes 589840 | tf_op jit(solution)/shard_map/reduce_scatter | solution.py:305
  457.8 135.0 %all-reduce.5.cloned.1.call-done = (f32[1024,128]{1,0:T(8,128)}, f32[128,1024]{1,0:T(8,128)}, f32[1024,128]{1,0:T(8,128)}, f32[128,1024]{1,0:T(8,128)}) async-done(((f32[1024,128]{1,0:T(8,128)}, f32[128,1024]{1,0:T(8,128)}, f32[1024,128]{1,0:T(8,128)}, f32[128,1024]{1,0:T(8,128)}), (f32[1024,128]{1,0:T(8,128)}, f32[128,1024]{1,0:T(8,128)}, f32[1024,128]{1,0:T(8,128)}, ...) | async-done | bytes 2097168 | tf_op jit(solution)/shard_map/psum | solution.py:318
  592.8 1.9 copy.136
  594.6 1.9 copy.137
  596.5 1.9 copy.138
  598.4 1.9 copy.139
  (263 shorter events, 64.5 us)
Async XLA Ops:
  7.2 148.2 %copy-start = (bf16[1024,128]{1,0:T(8,128)(2,1)S(1)}, bf16[1024,128]{1,0:T(8,128)(2,1)}, u32[]{:S(2)}) copy-start(bf16[1024,128]{1,0:T(8,128)(2,1)} %param.52) | copy-start | bytes 786436
  7.2 31.6 %all-gather.7.cloned.1.call-start = ((), (), s32[]{:S(2)}) async-start(), calls=%async_computation.4 | async-start | bytes 2621440 | tf_op jit(solution)/shard_map/all_gather | solution.py:205
  8.5 30.4 %copy-start.37 = (f32[256]{0:T(256)}, f32[256]{0:T(256)S(1)}, u32[]{:S(2)}) copy-start(f32[256]{0:T(256)S(1)} %broadcast_multiply_fusion.1) | copy-start | bytes 3076
  9.8 29.0 %copy-start.55 = (f32[256]{0:T(256)}, f32[256]{0:T(256)S(1)}, u32[]{:S(2)}) copy-start(f32[256]{0:T(256)S(1)} %fusion.103) | copy-start | bytes 3076
  9.8 29.0 %copy-start.45 = (f32[256]{0:T(256)}, f32[256]{0:T(256)S(1)}, u32[]{:S(2)}) copy-start(f32[256]{0:T(256)S(1)} %fusion.138) | copy-start | bytes 3076
  12.0 112.0 %reduce-scatter.5.cloned.1.call-start = ((), (), s32[]{:S(2)}) async-start(), calls=%async_computation.5 | async-start | bytes 2949120 | tf_op jit(solution)/shard_map/reduce_scatter | solution.py:216
  12.8 4.3 copy-start.43
  17.2 14.0 %copy-start.58 = (s32[128]{0:T(128)}, s32[128]{0:T(128)S(1)}, u32[]{:S(2)}) copy-start(s32[128]{0:T(128)S(1)} %and_select_fusion) | copy-start | bytes 1540
  18.5 24.2 %copy-start.35 = (s32[1024]{0:T(1024)}, s32[1024]{0:T(1024)S(1)}, u32[]{:S(2)}) copy-start(s32[1024]{0:T(1024)S(1)} %fusion.125) | copy-start | bytes 12292
  29.1 13.6 %copy-start.19 = (bf16[1024,128]{1,0:T(8,128)(2,1)}, bf16[1024,128]{1,0:T(8,128)(2,1)S(1)}, u32[]{:S(2)}) copy-start(bf16[1024,128]{1,0:T(8,128)(2,1)S(1)} %all_gather.35) | copy-start | bytes 786436
  31.2 25.0 %copy-start.49 = (pred[1024]{0:T(1024)(128)(4,1)}, pred[1024]{0:T(1024)(128)(4,1)S(1)}, u32[]{:S(2)}) copy-start(pred[1024]{0:T(1024)(128)(4,1)S(1)} %compare_and_fusion) | copy-start | bytes 3076
  31.9 10.8 %copy-start.33 = (bf16[128,3,256]{2,0,1:T(8,128)(2,1)S(1)}, bf16[128,3,256]{2,0,1:T(8,128)(2,1)}, u32[]{:S(2)}) copy-start(bf16[128,3,256]{2,0,1:T(8,128)(2,1)} %param.49) | copy-start | bytes 589828
  56.2 9.2 %copy-start.64 = (s32[1,2]{1,0:T(1,128)S(1)}, s32[1,2]{1,0:T(1,128)}, u32[]{:S(2)}) copy-start(s32[1,2]{1,0:T(1,128)} %param.33) | copy-start | bytes 28
  81.3 4.7 copy-start.29
  89.0 34.9 %copy-start.2 = (bf16[256,1024]{1,0:T(8,128)(2,1)S(1)}, bf16[256,1024]{1,0:T(8,128)(2,1)}, u32[]{:S(2)}) copy-start(bf16[256,1024]{1,0:T(8,128)(2,1)} %param.31) | copy-start | bytes 1572868
  90.8 58.0 %all-gather.11.cloned.1.call-start = ((), (), s32[]{:S(2)}) async-start(), calls=%async_computation.8 | async-start | bytes 2621440 | tf_op jit(solution)/shard_map/all_gather | solution.py:248
  91.7 81.8 %all-gather.9.cloned.1.call-start = ((), (), s32[]{:S(2)}) async-start(), calls=%async_computation.6 | async-start | bytes 2621440 | tf_op jit(solution)/shard_map/all_gather | solution.py:227
  127.6 96.3 %reduce-scatter.9.cloned.1.call-start = ((), (), s32[]{:S(2)}) async-start(), calls=%async_computation.9 | async-start | bytes 2949120 | tf_op jit(solution)/shard_map/reduce_scatter | solution.py:267
  135.5 19.8 %copy-start.15 = (bf16[256,1024]{1,0:T(8,128)(2,1)S(1)}, bf16[256,1024]{1,0:T(8,128)(2,1)}, u32[]{:S(2)}) copy-start(bf16[256,1024]{1,0:T(8,128)(2,1)} %add_convert_fusion.1) | copy-start | bytes 1572868
  161.4 16.6 %copy-start.31 = (bf16[128,1024]{1,0:T(8,128)(2,1)S(1)}, bf16[128,1024]{1,0:T(8,128)(2,1)}, u32[]{:S(2)}) copy-start(bf16[128,1024]{1,0:T(8,128)(2,1)} %param.53) | copy-start | bytes 786436
  173.5 4.6 copy-start.60
  178.1 2.9 copy-start.32
  178.1 3.9 copy-start.67
  182.0 4.6 copy-start.62
  190.7 35.7 %copy-start.57 = (f32[256]{0:T(256)S(1)}, f32[256]{0:T(256)}, u32[]{:S(2)}) copy-start(f32[256]{0:T(256)} %copy-done.56) | copy-start | bytes 3076
  190.7 35.7 %copy-start.41 = (f32[256]{0:T(256)S(1)}, f32[256]{0:T(256)}, u32[]{:S(2)}) copy-start(f32[256]{0:T(256)} %copy-done.40) | copy-start | bytes 3076
  190.7 35.7 %copy-start.54 = (f32[256]{0:T(256)S(1)}, f32[256]{0:T(256)}, u32[]{:S(2)}) copy-start(f32[256]{0:T(256)} %copy-done.53) | copy-start | bytes 3076
  190.8 63.1 %all-gather.13.cloned.1.call-start = ((), (), s32[]{:S(2)}) async-start(), calls=%async_computation.10 | async-start | bytes 2621440 | tf_op jit(solution)/shard_map/all_gather | solution.py:284
  224.0 3.9 copy-start.7
  226.9 8.7 %copy-start.51 = (f32[256]{0:T(256)}, f32[256]{0:T(256)S(1)}, u32[]{:S(2)}) copy-start(f32[256]{0:T(256)S(1)} %negate_multiply_fusion.1) | copy-start | bytes 3076
  228.9 150.6 %reduce-scatter.7.cloned.1.call-start = ((), (), s32[]{:S(2)}) async-start(), calls=%async_computation.7 | async-start | bytes 2949120 | tf_op jit(solution)/shard_map/reduce_scatter | solution.py:236
  238.1 147.7 %all-reduce.7.cloned.1.call-start = ((), (), s32[]{:S(2)}) async-start(), calls=%async_computation.14 | async-start | bytes 1179648 | tf_op jit(solution)/shard_map/psum | solution.py:324
  241.6 4.8 copy-start.12
  241.6 4.8 copy-start.26
  241.6 10.9 %copy-start.23 = (bf16[1024,256]{1,0:T(8,128)(2,1)S(1)}, bf16[1024,256]{1,0:T(8,128)(2,1)}, u32[]{:S(2)}) copy-start(bf16[1024,256]{1,0:T(8,128)(2,1)} %copy-done.22) | copy-start | bytes 1572868
  241.6 10.9 %copy-start.47 = (pred[1024]{0:T(1024)(128)(4,1)S(1)}, pred[1024]{0:T(1024)(128)(4,1)}, u32[]{:S(2)}) copy-start(pred[1024]{0:T(1024)(128)(4,1)} %compare_and_fusion.1) | copy-start | bytes 3076
  253.7 162.1 %all-gather.15.cloned.1.call-start = ((), (), s32[]{:S(2)}) async-start(), calls=%async_computation.12 | async-start | bytes 1769472 | tf_op jit(solution)/shard_map/all_gather | solution.py:16
  257.4 7.6 %copy-start.50 = (pred[1024]{0:T(1024)(128)(4,1)S(1)}, pred[1024]{0:T(1024)(128)(4,1)}, u32[]{:S(2)}) copy-start(pred[1024]{0:T(1024)(128)(4,1)} %copy-done.49) | copy-start | bytes 3076
  266.1 5.1 copy-start.65
  285.5 11.7 %copy-start.66 = (s32[2]{0:T(128)S(1)}, s32[2]{0:T(128)}, u32[]{:S(2)}) copy-start(s32[2]{0:T(128)} %copy-done.65) | copy-start | bytes 28 | tf_op jit(solution)/shard_map/while
  297.1 5.1 copy-start.65
  316.4 11.6 %copy-start.66 = (s32[2]{0:T(128)S(1)}, s32[2]{0:T(128)}, u32[]{:S(2)}) copy-start(s32[2]{0:T(128)} %copy-done.65) | copy-start | bytes 28 | tf_op jit(solution)/shard_map/while
  328.0 13.4 %copy-start.30 = (bf16[2,512,4,64]{1,3,2,0:T(8,128)(2,1)S(1)}, bf16[2,512,4,64]{1,3,2,0:T(8,128)(2,1)}, u32[]{:S(2)}) copy-start(bf16[2,512,4,64]{1,3,2,0:T(8,128)(2,1)} %get-tuple-element.261) | copy-start | bytes 1572868
  341.4 12.0 %copy-start.39 = (s32[1024]{0:T(1024)S(1)}, s32[1024]{0:T(1024)}, u32[]{:S(2)}) copy-start(s32[1024]{0:T(1024)} %get-tuple-element.325) | copy-start | bytes 12292
  347.6 16.0 %copy-start.48 = (pred[1024]{0:T(1024)(128)(4,1)S(1)}, pred[1024]{0:T(1024)(128)(4,1)}, u32[]{:S(2)}) copy-start(pred[1024]{0:T(1024)(128)(4,1)} %compare_and_fusion.1) | copy-start | bytes 3076
  353.4 16.9 %copy-start.20 = (bf16[1024,128]{1,0:T(8,128)(2,1)S(1)}, bf16[1024,128]{1,0:T(8,128)(2,1)}, u32[]{:S(2)}) copy-start(bf16[1024,128]{1,0:T(8,128)(2,1)} %copy-done.19) | copy-start | bytes 786436
  363.6 8.1 %copy-start.34 = (bf16[128,3,256]{2,0,1:T(8,128)(2,1)S(1)}, bf16[128,3,256]{2,0,1:T(8,128)(2,1)}, u32[]{:S(2)}) copy-start(bf16[128,3,256]{2,0,1:T(8,128)(2,1)} %param.49) | copy-start | bytes 589828
  371.4 6.2 %copy-start.13 = (bf16[256,1024]{1,0:T(8,128)(2,1)S(1)}, bf16[256,1024]{1,0:T(8,128)(2,1)}, u32[]{:S(2)}) copy-start(bf16[256,1024]{1,0:T(8,128)(2,1)} %fusion.116) | copy-start | bytes 1572868
  371.4 8.1 %copy-start.11 = (bf16[256,1024]{1,0:T(8,128)(2,1)S(1)}, bf16[256,1024]{1,0:T(8,128)(2,1)}, u32[]{:S(2)}) copy-start(bf16[256,1024]{1,0:T(8,128)(2,1)} %convert_element_type.133) | copy-start | bytes 1572868
  371.4 78.7 %reduce-scatter.11.cloned.1.call-start = ((), (), s32[]{:S(2)}) async-start(), calls=%async_computation.11 | async-start | bytes 2949120 | tf_op jit(solution)/shard_map/reduce_scatter | solution.py:305
  377.5 3.9 copy-start.16
  377.5 6.0 copy-start.27
  377.5 6.0 copy-start.61
  377.5 215.3 %all-reduce.5.cloned.1.call-start = ((), (), s32[]{:S(2)}) async-start(), calls=%async_computation.13 | async-start | bytes 4194304 | tf_op jit(solution)/shard_map/psum | solution.py:318
  383.5 68.8 %copy-start.14 = (bf16[256,1024]{1,0:T(8,128)(2,1)S(1)}, bf16[256,1024]{1,0:T(8,128)(2,1)}, u32[]{:S(2)}) copy-start(bf16[256,1024]{1,0:T(8,128)(2,1)} %fusion.106) | copy-start | bytes 1572868
  389.1 64.3 %copy-start.3 = (bf16[256,1024]{1,0:T(8,128)(2,1)S(1)}, bf16[256,1024]{1,0:T(8,128)(2,1)}, u32[]{:S(2)}) copy-start(bf16[256,1024]{1,0:T(8,128)(2,1)} %param.31) | copy-start | bytes 1572868
  389.2 64.3 %copy-start.28 = (bf16[1024,128]{1,0:T(8,128)(2,1)S(1)}, bf16[1024,128]{1,0:T(8,128)(2,1)}, u32[]{:S(2)}) copy-start(bf16[1024,128]{1,0:T(8,128)(2,1)} %param.48) | copy-start | bytes 786436
  389.2 64.3 %copy-start.38 = (f32[256]{0:T(256)S(1)}, f32[256]{0:T(256)}, u32[]{:S(2)}) copy-start(f32[256]{0:T(256)} %copy-done.37) | copy-start | bytes 3076
  389.2 64.3 %copy-start.42 = (f32[1024]{0:T(1024)S(1)}, f32[1024]{0:T(1024)}, u32[]{:S(2)}) copy-start(f32[1024]{0:T(1024)} %param.36) | copy-start | bytes 12292
  417.5 38.4 %copy-start.46 = (f32[256]{0:T(256)S(1)}, f32[256]{0:T(256)}, u32[]{:S(2)}) copy-start(f32[256]{0:T(256)} %copy-done.45) | copy-start | bytes 3076
  418.3 38.1 %copy-start.8 = (f32[256,1024]{1,0:T(8,128)S(1)}, f32[256,1024]{1,0:T(8,128)}, u32[]{:S(2)}) copy-start(f32[256,1024]{1,0:T(8,128)} %param.32) | copy-start | bytes 3145732
  418.3 38.1 %copy-start.10 = (f32[256,1024]{1,0:T(8,128)S(1)}, f32[256,1024]{1,0:T(8,128)}, u32[]{:S(2)}) copy-start(f32[256,1024]{1,0:T(8,128)} %copy-done.9) | copy-start | bytes 3145732
  418.3 38.1 %copy-start.52 = (f32[256]{0:T(256)S(1)}, f32[256]{0:T(256)}, u32[]{:S(2)}) copy-start(f32[256]{0:T(256)} %copy-done.51) | copy-start | bytes 3076
  456.3 143.9 %copy-start.1 = (bf16[1024,128]{1,0:T(8,128)(2,1)S(1)}, bf16[1024,128]{1,0:T(8,128)(2,1)}, u32[]{:S(2)}) copy-start(bf16[1024,128]{1,0:T(8,128)(2,1)} %param.52) | copy-start | bytes 786436
  (19 other events, 35.5 us)
Sparse Core Ops, SparseCore 0:
  12.1 26.6 all-gather.6
  90.9 33.0 reduce-scatter.4
  126.2 22.5 all-gather.10
  150.9 22.5 all-gather.8
  190.9 33.0 reduce-scatter.8
  229.0 22.7 all-gather.12
  254.4 33.0 reduce-scatter.6
  292.2 73.4 all-reduce.6
  371.5 44.2 all-gather.14
  418.2 31.8 reduce-scatter.10
  457.9 134.8 all-reduce.4
